TPU v7x, 512 devices: a whole 4x8x8 slice. The times are simulated.
512 devices in a mesh: illum: 32 (over z, y_hi), slab: 8 (over x, core), cuts: 2 (over y_lo).
Axes of the slice: x: 4, y: 8 (y_hi: 4, y_lo: 2; y = y_hi * 2 + y_lo), z: 8, core: 2. Of those that a mesh axis runs over, the one named last changes fastest.
Arguments:
- phase_delay: float32 [4, 256, 1024], P('cuts', 'slab', 'illum'), may hold values from -1.5 to 1.5
- attenuation: float32 [4, 256, 1024], P('cuts', 'slab', 'illum'), may hold values from 0.02 to 0.3
- measured: float32 [32, 2, 256, 1024], P('illum', None, 'slab'), may hold values from -6 to 6
- angles: int32 [32, 2], P('illum'), may hold values from -16 to 16
Outputs:
- grad_phase: float32 [4, 256, 1024], P('cuts', 'slab', 'illum')
- grad_atten: float32 [4, 256, 1024], P('cuts', 'slab', 'illum')
All inputs are finite; a program needn't handle non-finite values.
Results may differ from a plain program's by a relative error of at most 0.0001.
Values sent between devices are 32-bit elements; how exact they have to be, the bound alone decides.
No kernel may reach another device: no remote copies, remote signals or barrier semaphores. Data moves between devices by JAX's collectives and lax.ppermute only.
A program may use at most 64 MiB of HBM per device.

v0:
```python
import functools
import math

import jax
import jax.numpy as jnp
from jax import lax
from jax.experimental import pallas as pl
from jax.experimental.pallas import tpu as pltpu
from jax.sharding import PartitionSpec as P


step_coeff = 0.08
square_coeff = 0.0032
ratio = step_coeff / square_coeff
two_pi = 2.0 * math.pi

HALO = 8
REACH = 16
VMEM = pl.BlockSpec(memory_space=pltpu.VMEM)
SMEM = pl.BlockSpec(memory_space=pltpu.SMEM)
HBM = pl.BlockSpec(memory_space=pltpu.HBM)
small = pltpu.CompilerParams(vmem_limit_bytes=1 << 20)
large = pltpu.CompilerParams(vmem_limit_bytes=8 << 20)


def f32(*shape):
    return jax.ShapeDtypeStruct(shape, jnp.float32)


def lanes_of(shape):
    return lax.broadcasted_iota(jnp.int32, shape, 1)


def turn(x, by):
    by %= 128
    return pltpu.roll(x, by, 1) if by else x


def pack_object(
    phase_ref, atten_ref, measured_ref, angles_ref,
    out_ref, whole_ref, head_ref,
    phase, atten, turns, sems,
):
    copies = [
        pltpu.make_async_copy(phase_ref, phase, sems.at[0]),
        pltpu.make_async_copy(atten_ref, atten, sems.at[1]),
        pltpu.make_async_copy(angles_ref, turns, sems.at[2]),
        pltpu.make_async_copy(measured_ref.at[0], whole_ref, sems.at[3]),
    ]
    for copy in copies:
        copy.start()
    for copy in copies[:3]:
        copy.wait()
    for n, (ref, layer) in enumerate(((phase, 0), (phase, 1), (atten, 0), (atten, 1))):
        out_ref[:, 32 * n : 32 * n + 32] = ref[layer]
    lane = lanes_of((8, 128))
    head_ref[...] = jnp.where(lane == 0, turns[0, 0], turns[0, 1]).astype(jnp.float32)
    copies[3].wait()


def pairs_of(first, mine_ref, other_ref, rows):
    mine, other = mine_ref[rows], other_ref[rows]
    return [jnp.where(first, mine, other), jnp.where(first, other, mine)]


def sides_of(first, near_ref, far_ref, rows):
    near, far = near_ref[rows], far_ref[rows]
    return [jnp.where(first, near, far), jnp.where(first, far, near)]


def pack_sides(place_ref, mine_ref, other_ref, out_ref):
    first = place_ref[2] == 0
    lane = lanes_of((8, 128))
    spots = 32 * jnp.bitwise_and(lane // 16, 3) + jnp.bitwise_and(lane, 15)
    for block in range(4):
        rows = slice(8 * block, 8 * block + 8)
        both = pairs_of(first, mine_ref, other_ref, rows)
        left, right = (
            jnp.where(lane < 64, *(picked(x, spots + shift) for x in both)) for shift in (0, 16)
        )
        out_ref[rows] = jnp.where(first, left, right)


def pack_edges(place_ref, mine_ref, other_ref, near_ref, across_ref, along_ref):
    first = place_ref[2] == 0
    top, bottom = (
        pairs_of(first, mine_ref, other_ref, rows) + [near_ref[rows]]
        for rows in (slice(0, 8), slice(24, 32))
    )
    for k in range(3):
        across_ref[k] = jnp.where(first, top[k], bottom[k])
    along_ref[...] = jnp.where(first, bottom[2], top[2])


def pack_rows(
    place_ref, mine_ref, other_ref, near_ref, far_ref, across_ref, along_ref,
    out_ref, left_ref, right_ref,
):
    first = place_ref[2] == 0
    near_edge, far_edge = along_ref[...], across_ref[2]
    edges = [
        across_ref[0],
        across_ref[1],
        jnp.where(first, near_edge, far_edge),
        jnp.where(first, far_edge, near_edge),
    ]
    blocks = []
    for block in range(4):
        rows = slice(8 * block, 8 * block + 8)
        blocks.append(
            pairs_of(first, mine_ref, other_ref, rows)
            + sides_of(first, near_ref, far_ref, rows)
        )
    for block in range(4):
        rows = slice(8 * block, 8 * block + 8)
        new = []
        for k in range(4):
            above = blocks[block - 1][k] if block else edges[k]
            below = blocks[block + 1][k] if block < 3 else edges[k]
            new.append(jnp.where(first, above, below))
        out_ref[0, rows], out_ref[1, rows], left_ref[rows], right_ref[rows] = new


def flipped(x):
    rows = 7 - lax.broadcasted_iota(jnp.int32, (8, 128), 0)
    return jnp.take_along_axis(x, rows, axis=0)


def picked(x, lanes):
    return jnp.take_along_axis(x, lanes, axis=1)


def thirds(x):
    parts = []
    for _ in range(3):
        part = x.astype(jnp.bfloat16)
        x = x - part.astype(jnp.float32)
        parts.append(part)
    return jnp.concatenate(parts, axis=1)


def permuted(x, chosen):
    ones = jnp.where(chosen, 1.0, 0.0).astype(jnp.bfloat16)
    return jnp.dot(
        thirds(x),
        jnp.concatenate([ones] * 3, axis=0),
        preferred_element_type=jnp.float32,
    )


def square_iotas(width=128):
    shape = (128, width)
    return lax.broadcasted_iota(jnp.int32, shape, 0), lanes_of(shape)


def pack_measured(place_ref, whole_ref, head_ref, out_ref, plain, packed, sems):
    lane = lanes_of((8, 128))
    head = head_ref[...]
    zero = jnp.zeros((8, 128), jnp.float32)
    source, target = square_iotas()
    m = jnp.bitwise_and(target // 16 - jnp.tile(place_ref[0] // 8, (16, 1)), 3)
    chosen = source == jnp.bitwise_and(target, 64) + 4 * jnp.bitwise_and(target, 15) + m
    cut = place_ref[2]
    regs = []
    for comp in range(2):
        rows = []
        for a in range(2):
            rows.append([])
            for n in range(8):
                at = slice(128 * n, 128 * n + 128)
                x = jnp.where(
                    cut == 0,
                    whole_ref[comp, 8 * a : 8 * a + 8, at],
                    whole_ref[comp, 8 * a + 16 : 8 * a + 24, at],
                )
                rows[a].append(flipped(x) if a else x)
        regs.append(rows)
    copies = []
    for j in range(32):
        v, r = divmod(32 * j - REACH, 128)
        for comp in range(2):
            parts = []
            for a in range(2):
                left = regs[comp][a][v] if v >= 0 else zero
                part = turn(left, 64 * a - r)
                if r > 64:
                    right = regs[comp][a][v + 1] if v + 1 < 8 else zero
                    part = jnp.where(lane - 64 * a < 128 - r, part, turn(right, 64 * a - r))
                parts.append(part)
            both = jnp.where(lane < 64, parts[0], parts[1])
            if comp == 0:
                both = jnp.where(lane < 2, head, both)
            plain[16 * j + 8 * comp : 16 * j + 8 * comp + 8] = both
        if j % 8 == 7:
            part = pl.ds(j - 7, 8)
            moved = permuted(plain[16 * j - 112 : 16 * j + 16], chosen)
            packed[part] = moved.reshape(8, 16, 128)
            copies.append(
                pltpu.make_async_copy(packed.at[part], out_ref.at[part], sems.at[j // 8])
            )
            copies[-1].start()
    for copy in copies:
        copy.wait()


def march(
    place_ref, here_ref, left_ref, right_ref, got_ref,
    mine_ref, other_ref, edge_ref,
    table, flat, field, stored, sums,
):
    block, slab, cut = place_ref[0], place_ref[1], place_ref[2]
    first = cut == 0
    lane = lanes_of((8, 128))
    sub = lax.broadcasted_iota(jnp.int32, (8, 128), 0)
    upper = lane < 64
    window = jnp.bitwise_and(lane, 63)
    half = jnp.bitwise_and(lane, 64)
    place = jnp.bitwise_and(lane, 15)
    group = jnp.bitwise_and(lane // 16, 3)
    top = 32 * slab + 16 * cut - HALO
    left_column = 32 * block - REACH

    def columns(m):
        return left_column + 4 * place + m

    for q in range(2):
        row = top + jnp.where(upper, 8 * q + sub, 31 - 8 * q - sub)
        row_inside = (row >= 0) & (row < 256)
        column = left_column + window
        inside = row_inside & (column >= 0) & (column < 1024)
        for m in range(4):
            column = columns(m)
            table[8, m, 8 * q : 8 * q + 8] = jnp.where(
                row_inside & (column >= 0) & (column < 1024), square_coeff, 0.0
            )
        for layer in range(4):
            pair, sl = divmod(layer, 2)
            values = []
            for n in (sl, 2 + sl):
                halves = []
                for a, b in ((0, q), (1, 3 - q)):
                    rows = slice(8 * b, 8 * b + 8)
                    at = 64 * (a - pair) - 16 * n
                    halves.append(
                        jnp.where(
                            window < 16,
                            turn(left_ref[rows], at),
                            jnp.where(
                                window < 48,
                                turn(here_ref[pair, rows], 64 * a - 32 * n + 16),
                                turn(right_ref[rows], at + 48),
                            ),
                        )
                    )
                values.append(jnp.where(upper, halves[0], flipped(halves[1])))
            damping = jnp.where(inside, jnp.exp(-values[1]), 0.0)
            re, im = damping * jnp.cos(values[0]), damping * jnp.sin(values[0])
            flat[32 * layer + 8 * q : 32 * layer + 8 * q + 8] = re
            flat[32 * layer + 8 * q + 16 : 32 * layer + 8 * q + 24] = im
    source, target = square_iotas(512)
    spot = jnp.bitwise_and(target, 64) + 4 * jnp.bitwise_and(target, 15) + target // 128
    wide = permuted(flat[...], source == spot)
    for m in range(4):
        table[0:8, m] = wide[:, 128 * m : 128 * m + 128].reshape(8, 16, 128)

    def spread(n, m, r):
        return jnp.broadcast_to(table[n, m, r : r + 1], (8, 128))

    def side(x, m):
        before = x[m - 1] if m else turn(x[3], 1)
        after = x[m + 1] if m < 3 else turn(x[0], 127)
        return before + after

    def diffract(source, begin, inner, orient, emit):
        rows, scaled = {}, {}

        def around(values, r, k, m):
            parts = [values[n][k][m] for n in (r - 1, r + 1) if n in values]
            if r in values:
                parts.append(side(values[r][k], m))
            return functools.reduce(lambda x, y: x + y, parts)

        def scale(r):
            out = []
            for k in range(2):
                new = []
                for m in range(4):
                    total = around(rows, r, k, m)
                    if r in rows:
                        total = total - 4.0 * rows[r][k][m]
                    new.append(spread(8, m, r) * total)
                out.append(new)
            scaled[r] = out

        def finish(r):
            for m in range(4):
                re, im = (around(scaled, r, k, m) for k in range(2))
                if r in rows:
                    re, im = rows[r][0][m] - re, rows[r][1][m] - im
                else:
                    re, im = -re, -im
                if r in scaled:
                    mre, mim = scaled[r][0][m], scaled[r][1][m]
                    turned = orient * ratio
                    re = re + (4.0 * mre - turned * mim)
                    im = im + (4.0 * mim + turned * mre)
                emit(r, m, re, im)

        def advance(r):
            if r - 1 >= begin + inner:
                scale(r - 1)
            if r - 2 >= begin + 2 * inner:
                finish(r - 2)

        def opposite(row):
            return [[turn(x, 64) for x in part] for part in row]

        for r in range(begin, 16):
            rows[r] = source(r)
            advance(r)
        rows[16] = opposite(rows[15])
        advance(16)
        scaled[16] = opposite(scaled[15])
        finish(15)

    def received(comp, k):
        parts = [
            got_ref[pl.ds(128 * n + 8 * comp + k, 8, stride=16), :] for n in range(4)
        ]
        out = []
        for m in range(4):
            x = parts[3]
            for n in range(3):
                x = jnp.where(group == (m + n) % 4, parts[n], x)
            if m:
                x = picked(x, half + 16 * jnp.bitwise_and(group + m, 3) + place)
            out.append(x)
        return out

    head = received(0, 0)
    corner = jnp.bitwise_and(lane, 48)
    row_turns = picked(head[0], corner)
    col_turns = picked(head[1], corner)
    row0 = (top + jnp.where(upper, 0, 31)).astype(jnp.float32)
    row_part = row_turns * row0 * (1.0 / 256.0)
    col_part = col_turns * columns(0).astype(jnp.float32) * (1.0 / 1024.0)
    row_part = row_part - jnp.floor(row_part)
    col_part = col_part - jnp.floor(col_part)

    def unit(t):
        return jnp.cos(t), jnp.sin(t)

    def times(a, b):
        return a[0] * b[0] - a[1] * b[1], a[0] * b[1] + a[1] * b[0]

    wave = [unit(two_pi * (row_part + col_part))]
    step = unit(two_pi / 256.0 * row_turns * jnp.where(upper, 1.0, -1.0))
    across = unit(two_pi / 1024.0 * col_turns)
    for _ in range(3):
        wave.append(times(wave[-1], across))
    waves = [wave]

    def from_wave(r):
        while len(waves) <= r:
            waves.append([times(x, step) for x in waves[-1]])
        return [[x[k] for x in waves[r]] for k in range(2)]

    def from_field(r):
        return [[field[k, r, m] for m in range(4)] for k in range(2)]

    def forward(layer):
        def source(r):
            re, im = from_wave(r) if layer == 0 else from_field(r)
            out = ([], [])
            for m in range(4):
                v = times((spread(2 * layer, m, r), spread(2 * layer + 1, m, r)), (re[m], im[m]))
                for k in range(2):
                    stored[2 * layer + k, r, m] = v[k]
                    out[k].append(v[k])
            return out

        measured_rows = {}

        def emit(r, m, re, im):
            if layer < 3:
                field[0, r, m], field[1, r, m] = re, im
                return
            if r not in measured_rows:
                measured_rows[r] = [received(k, r - 8) for k in range(2)]
            column = columns(m)
            keep = (column >= 0) & (column < 1024)
            field[0, r, m] = jnp.where(keep, re - measured_rows[r][0][m], 0.0)
            field[1, r, m] = jnp.where(keep, im - measured_rows[r][1][m], 0.0)

        diffract(source, 2 * layer, 1, 1.0, emit)

    def backward(layer):
        def emit(r, m, re, im):
            vre, vim = stored[2 * layer, r, m], stored[2 * layer + 1, r, m]
            for out, x in enumerate((vre * im - vim * re, vre * re + vim * im)):
                sums[2 * layer + out, m, r : r + 1] = jnp.sum(x, axis=0, keepdims=True)
            if layer:
                a, b = spread(2 * layer, m, r), spread(2 * layer + 1, m, r)
                field[0, r, m], field[1, r, m] = a * re + b * im, a * im - b * re

        diffract(from_field, 2 * layer + 2, -1, -1.0, emit)

    for layer in range(4):
        forward(layer)
        for n in range(2):
            for m in range(4):
                if layer:
                    sums[2 * layer + n, m, 0 : 2 * layer] = jnp.zeros((2 * layer, 128))
    for layer in (3, 2, 1, 0):
        backward(layer)

    source, target = square_iotas()
    near = (jnp.bitwise_and(source, 64) == jnp.bitwise_and(target, 64)) & (
        jnp.bitwise_and(source, 15) == jnp.bitwise_and(target, 63) // 4
    )
    total = None
    for m in range(4):
        x = sums[:, m].reshape(128, 128)
        x = permuted(x, near & (jnp.bitwise_and(target, 3) == m))
        total = x if total is None else total + x
    flat[...] = total

    def plain(n, q):
        return flat[16 * n + 8 * q : 16 * n + 8 * q + 8]

    blocks = [[None] * 4 for _ in range(2)]
    for pair in range(2):
        for q in range(2):
            for n in range(4):
                out, sl = divmod(n, 2)
                x = plain(2 * (2 * pair + sl) + out, q)
                x = -x if out else x
                for b, y in ((q, turn(x, 32 * n - 16)), (3 - q, turn(x, 32 * n - 80))):
                    old = blocks[pair][b]
                    blocks[pair][b] = y if old is None else jnp.where(lane < 32 * n, old, y)
        for b in (2, 3):
            blocks[pair][b] = flipped(blocks[pair][b])
    mine = [jnp.where(first, a, b) for a, b in zip(*blocks)]
    other = [jnp.where(first, b, a) for a, b in zip(*blocks)]
    none = jnp.zeros((8, 128), jnp.float32)
    for parts, ref in ((mine, mine_ref), (other, other_ref)):
        for b in range(4):
            ref[8 * b : 8 * b + 8] = jnp.where(
                first, parts[b + 1] if b < 3 else none, parts[b - 1] if b > 0 else none
            )
    for pair in range(2):
        edge_ref[pair] = jnp.where(first, blocks[pair][0], blocks[pair][3])


def add_edges(place_ref, other_ref, edge_ref, out_ref):
    first = place_ref[2] == 0
    edge = jnp.where(first, edge_ref[1], edge_ref[0])
    none = jnp.zeros((8, 128), jnp.float32)
    out_ref[0:8] = other_ref[0:8] + jnp.where(first, edge, none)
    out_ref[8:24] = other_ref[8:24]
    out_ref[24:32] = other_ref[24:32] + jnp.where(first, none, edge)


def combine(place_ref, mine_ref, other_ref, edge_ref, phase_ref, atten_ref):
    first = place_ref[2] == 0
    edge = jnp.where(first, edge_ref[0], edge_ref[1])
    for b in range(4):
        rows = slice(8 * b, 8 * b + 8)
        total = mine_ref[rows] + other_ref[rows]
        if b == 0:
            total = total + jnp.where(first, edge, 0.0)
        if b == 3:
            total = total + jnp.where(first, 0.0, edge)
        for sl in range(2):
            phase_ref[sl, rows] = turn(total, -32 * sl)[:, 0:32]
            atten_ref[sl, rows] = turn(total, -64 - 32 * sl)[:, 0:32]


def body(phase_delay, attenuation, measured, angles):
    block = lax.axis_index("illum")
    slab = lax.axis_index("slab")
    cut = lax.axis_index("cuts")
    place = jnp.stack([jnp.full((8, 128), n, jnp.int32) for n in (block, slab, cut)])
    n_slabs, n_blocks = lax.axis_size("slab"), lax.axis_size("illum")
    rows_axis = ("slab", "cuts")

    def both_ways(pairs):
        return pairs + [(b, a) for a, b in pairs]

    partner = both_ways([(2 * s, 2 * s + 1) for s in range(n_slabs)])
    across = both_ways([(2 * s + 1, 2 * s + 2) for s in range(n_slabs - 1)])
    along = [(2 * s, 2 * s + 2) for s in range(n_slabs - 1)]
    along += [(2 * s + 3, 2 * s + 1) for s in range(n_slabs - 1)]
    beside = both_ways([(2 * i + 1, 2 * i + 2) for i in range(n_blocks - 1)])
    phase_delay, attenuation, measured, angles = (
        pltpu.with_memory_space_constraint(x, pltpu.HBM)
        for x in (phase_delay, attenuation, measured, angles)
    )
    mine, whole, head = pl.pallas_call(
        pack_object,
        out_shape=(f32(32, 128), f32(2, 32, 1024), f32(8, 128)),
        in_specs=[HBM] * 4,
        out_specs=(VMEM,) * 3,
        scratch_shapes=[
            pltpu.VMEM((2, 32, 32), jnp.float32),
            pltpu.VMEM((2, 32, 32), jnp.float32),
            pltpu.SMEM((1, 2), jnp.int32),
            pltpu.SemaphoreType.DMA((4,)),
        ],
        compiler_params=small,
    )(phase_delay, attenuation, measured, angles)
    other = lax.ppermute(mine, rows_axis, partner)
    sent = pl.pallas_call(
        pack_measured,
        out_shape=f32(32, 16, 128),
        in_specs=[VMEM] * 3,
        out_specs=HBM,
        scratch_shapes=[
            pltpu.VMEM((512, 128), jnp.float32),
            pltpu.VMEM((32, 16, 128), jnp.float32),
            pltpu.SemaphoreType.DMA((4,)),
        ],
        compiler_params=small,
    )(place, whole, head)
    near = pl.pallas_call(
        pack_sides,
        out_shape=f32(32, 128),
        in_specs=[VMEM] * 3,
        out_specs=VMEM,
        compiler_params=small,
    )(place, mine, other)
    near = lax.ppermute(near, ("illum", "cuts"), beside)
    got = lax.all_to_all(sent, "illum", 0, 0, tiled=True)
    far = lax.ppermute(near, rows_axis, partner)
    across_part, along_part = pl.pallas_call(
        pack_edges,
        out_shape=(f32(3, 8, 128), f32(8, 128)),
        in_specs=[VMEM] * 4,
        out_specs=(VMEM,) * 2,
        compiler_params=small,
    )(place, mine, other, near)
    across_part = lax.ppermute(across_part, rows_axis, across)
    along_part = lax.ppermute(along_part, rows_axis, along)
    here, from_left, from_right = pl.pallas_call(
        pack_rows,
        out_shape=(f32(2, 32, 128), f32(32, 128), f32(32, 128)),
        in_specs=[VMEM] * 7,
        out_specs=(VMEM,) * 3,
        compiler_params=small,
    )(place, mine, other, near, far, across_part, along_part)

    mine, other, edges = pl.pallas_call(
        march,
        out_shape=(f32(32, 128), f32(32, 128), f32(2, 8, 128)),
        in_specs=[VMEM] * 5,
        out_specs=(VMEM,) * 3,
        scratch_shapes=[
            pltpu.VMEM((9, 4, 16, 128), jnp.float32),
            pltpu.VMEM((128, 128), jnp.float32),
            pltpu.VMEM((2, 16, 4, 8, 128), jnp.float32),
            pltpu.VMEM((8, 16, 4, 8, 128), jnp.float32),
            pltpu.VMEM((8, 4, 16, 128), jnp.float32),
        ],
        compiler_params=large,
    )(place, here, from_left, from_right, got.reshape(512, 128))
    edges = lax.ppermute(edges, rows_axis, across)
    other = pl.pallas_call(
        add_edges,
        out_shape=f32(32, 128),
        in_specs=[VMEM] * 3,
        out_specs=VMEM,
        compiler_params=small,
    )(place, other, edges)
    other = lax.ppermute(other, rows_axis, partner)
    return pl.pallas_call(
        combine,
        out_shape=(f32(2, 32, 32), f32(2, 32, 32)),
        in_specs=[VMEM] * 4,
        out_specs=(VMEM, VMEM),
        compiler_params=small,
    )(place, mine, other, edges)


def solution(mesh):
    placed = (
        P("cuts", "slab", "illum"),
        P("cuts", "slab", "illum"),
        P("illum", None, "slab", None),
        P("illum", None),
    )
    return jax.shard_map(
        body,
        mesh=mesh,
        in_specs=placed,
        out_specs=(P("cuts", "slab", "illum"), P("cuts", "slab", "illum")),
        check_vma=False,
    )
```

profile of v0, /device:TPU:57, one launch (start us, length us, event | category | flops | bytes accessed | tf_op | source)
XLA Modules:
  0.0 59.6 jit_solution(11257521464550183731)
XLA Ops:
  0.6 0.1 add_add_fusion
  0.7 1.0 %shard_map.59 = (f32[32,128]{1,0:T(8,128)S(1)}, f32[2,32,1024]{2,1,0:T(8,128)S(1)}, f32[8,128]{1,0:T(8,128)S(1)}) custom-call(f32[2,32,32]{2,1,0:T(8,128)} %phase_ref.1, f32[2,32,32]{2,1,0:T(8,128)} %atten_ref.1, f32[1,2,32,1024]{3,2,1,0:T(8,128)} %measured_ref.1, s32[1,2]{1,0:T(1,128)} %angles_ref.1), custom_call_target="tpu_custom_call" | custom-call | tf_op jit(solution)/shard_map/pallas_call | solution.py:499
  1.7 0.1 broadcast.4.place_ref
  1.8 1.0 %shard_map.63 = f32[32,16,128]{2,1,0:T(8,128)} custom-call(s32[3,8,128]{2,1,0:T(8,128)S(1)} %broadcast.4.place_ref, f32[2,32,1024]{2,1,0:T(8,128)S(1)} %get-tuple-element.19.whole_ref, f32[8,128]{1,0:T(8,128)S(1)} %get-tuple-element.20.head_ref), custom_call_target="tpu_custom_call" | custom-call | tf_op jit(solution)/shard_map/pallas_call | solution.py:513
  2.8 15.1 %all-to-all-start = ((f32[32,16,128]{2,1,0:T(8,128)}), f32[32,16,128]{2,1,0:T(8,128)S(1)}, u32[]{:S(2)}, u32[]{:S(2)}) async-start(f32[32,16,128]{2,1,0:T(8,128)} %shard_map.63), calls=%async_computation | async-start | bytes 524288 | tf_op jit(solution)/shard_map/all_to_all | solution.py:533
  17.9 3.0 %collective-permute-start = (f32[32,128]{1,0:T(8,128)S(1)}, f32[32,128]{1,0:T(8,128)S(1)}, u32[]{:S(2)}, u32[]{:S(2)}) collective-permute-start(f32[32,128]{1,0:T(8,128)S(1)} %get-tuple-element.13.mine_ref), channel_id=1, source_target_pairs={{0,1},{2,3},{4,5},{6,7},{8,9},{10,11},{12,13},{14,15},{1,0},{3,2},... | collective-permute-start | bytes 49160 | tf_op jit(solution)/shard_map/ppermute | solution.py:512
  20.9 2.9 %collective-permute-done.other_ref = f32[32,128]{1,0:T(8,128)S(1)} collective-permute-done((f32[32,128]{1,0:T(8,128)S(1)}, f32[32,128]{1,0:T(8,128)S(1)}, u32[]{:S(2)}, u32[]{:S(2)}) %collective-permute-start) | collective-permute-done | bytes 16416 | tf_op jit(solution)/shard_map/ppermute | solution.py:512
  23.8 0.1 shard_map.60
  23.9 2.2 %collective-permute-start.1 = (f32[32,128]{1,0:T(8,128)S(1)}, f32[32,128]{1,0:T(8,128)S(1)}, u32[]{:S(2)}, u32[]{:S(2)}) collective-permute-start(f32[32,128]{1,0:T(8,128)S(1)} %shard_map.60), channel_id=1, source_target_pairs={{1,16},{17,32},{33,48},{49,64},{65,80},{81,96},{97,112},{113,128},... | collective-permute-start | bytes 49160 | tf_op jit(solution)/shard_map/ppermute | solution.py:532
  26.1 4.3 %collective-permute-done.1.near_ref = f32[32,128]{1,0:T(8,128)S(1)} collective-permute-done((f32[32,128]{1,0:T(8,128)S(1)}, f32[32,128]{1,0:T(8,128)S(1)}, u32[]{:S(2)}, u32[]{:S(2)}) %collective-permute-start.1) | collective-permute-done | bytes 16416 | tf_op jit(solution)/shard_map/ppermute | solution.py:532
  30.5 1.9 %collective-permute-start.2 = (f32[32,128]{1,0:T(8,128)S(1)}, f32[32,128]{1,0:T(8,128)S(1)}, u32[]{:S(2)}, u32[]{:S(2)}) collective-permute-start(f32[32,128]{1,0:T(8,128)S(1)} %collective-permute-done.1.near_ref), channel_id=1, source_target_pairs={{0,1},{2,3},{4,5},{6,7},{8,9},{10,11},{12,13},{14,15},{1,0},{3,2},... | collective-permute-start | bytes 49160 | tf_op jit(solution)/shard_map/ppermute | solution.py:534
  32.4 8.1 %collective-permute-start.3 = (f32[3,8,128]{2,1,0:T(8,128)S(1)}, f32[3,8,128]{2,1,0:T(8,128)S(1)}, u32[]{:S(2)}, u32[]{:S(2)}) collective-permute-start(f32[3,8,128]{2,1,0:T(8,128)S(1)} %get-tuple-element.14), channel_id=1, source_target_pairs={{1,2},{3,4},{5,6},{7,8},{9,10},{11,12},{13,14},{2,1},{4,3},{6,5},{... | collective-permute-start | bytes 36872 | tf_op jit(solution)/shard_map/ppermute | solution.py:542
  40.5 1.9 %collective-permute-start.4 = (f32[8,128]{1,0:T(8,128)S(1)}, f32[8,128]{1,0:T(8,128)S(1)}, u32[]{:S(2)}, u32[]{:S(2)}) collective-permute-start(f32[8,128]{1,0:T(8,128)S(1)} %get-tuple-element.15), channel_id=1, source_target_pairs={{0,2},{2,4},{4,6},{6,8},{8,10},{10,12},{12,14},{3,1},{5,3},{7,5},{... | collective-permute-start | bytes 12296 | tf_op jit(solution)/shard_map/ppermute | solution.py:543
  42.4 3.0 %collective-permute-done.4.along_ref = f32[8,128]{1,0:T(8,128)S(1)} collective-permute-done((f32[8,128]{1,0:T(8,128)S(1)}, f32[8,128]{1,0:T(8,128)S(1)}, u32[]{:S(2)}, u32[]{:S(2)}) %collective-permute-start.4) | collective-permute-done | bytes 4128 | tf_op jit(solution)/shard_map/ppermute | solution.py:543
  45.4 0.0 collective-permute-done.3.across_ref
  45.4 0.0 collective-permute-done.2.far_ref
  45.4 0.0 all-to-all-done
  45.4 3.1 %shard_map.64 = (f32[32,128]{1,0:T(8,128)S(1)}, f32[32,128]{1,0:T(8,128)S(1)}, f32[2,8,128]{2,1,0:T(8,128)S(1)}) custom-call(s32[3,8,128]{2,1,0:T(8,128)S(1)} %broadcast.4.place_ref, f32[2,32,128]{2,1,0:T(8,128)S(1)} %get-tuple-element.16.here_ref, f32[32,128]{1,0:T(8,128)S(1)} %get-tuple-element.17.left_ref, f32[32,128]{1,0:T(8,128)S(1)} %get-tuple-element.18.right_ref, ...), custom_call_target="tpu_custom_call" | custom-call | tf_op jit(solution)/shard_map/pallas_call | solution.py:552
  48.5 1.9 %collective-permute-start.5 = (f32[2,8,128]{2,1,0:T(8,128)S(1)}, f32[2,8,128]{2,1,0:T(8,128)S(1)}, u32[]{:S(2)}, u32[]{:S(2)}) collective-permute-start(f32[2,8,128]{2,1,0:T(8,128)S(1)} %get-tuple-element.23), channel_id=1, source_target_pairs={{1,2},{3,4},{5,6},{7,8},{9,10},{11,12},{13,14},{2,1},{4,3},{6,5},{... | collective-permute-start | bytes 24584 | tf_op jit(solution)/shard_map/ppermute | solution.py:566
  50.4 3.9 %collective-permute-done.5.edge_ref = f32[2,8,128]{2,1,0:T(8,128)S(1)} collective-permute-done((f32[2,8,128]{2,1,0:T(8,128)S(1)}, f32[2,8,128]{2,1,0:T(8,128)S(1)}, u32[]{:S(2)}, u32[]{:S(2)}) %collective-permute-start.5) | collective-permute-done | bytes 8224 | tf_op jit(solution)/shard_map/ppermute | solution.py:566
  54.4 1.9 %collective-permute-start.6 = (f32[32,128]{1,0:T(8,128)S(1)}, f32[32,128]{1,0:T(8,128)S(1)}, u32[]{:S(2)}, u32[]{:S(2)}) collective-permute-start(f32[32,128]{1,0:T(8,128)S(1)} %shard_map.65), channel_id=1, source_target_pairs={{0,1},{2,3},{4,5},{6,7},{8,9},{10,11},{12,13},{14,15},{1,0},{3,2},... | collective-permute-start | bytes 49160 | tf_op jit(solution)/shard_map/ppermute | solution.py:574
  56.3 2.6 %collective-permute-done.6.other_ref = f32[32,128]{1,0:T(8,128)S(1)} collective-permute-done((f32[32,128]{1,0:T(8,128)S(1)}, f32[32,128]{1,0:T(8,128)S(1)}, u32[]{:S(2)}, u32[]{:S(2)}) %collective-permute-start.6) | collective-permute-done | bytes 16416 | tf_op jit(solution)/shard_map/ppermute | solution.py:574
  58.8 0.7 %shard_map.66 = (f32[2,32,32]{2,1,0:T(8,128)}, f32[2,32,32]{2,1,0:T(8,128)}) custom-call(s32[3,8,128]{2,1,0:T(8,128)S(1)} %broadcast.4.place_ref, f32[32,128]{1,0:T(8,128)S(1)} %get-tuple-element.21.mine_ref, f32[32,128]{1,0:T(8,128)S(1)} %collective-permute-done.6.other_ref, f32[2,8,128]{2,1,0:T(8,128)S(1)} %collective-permute-done.5.edge_ref), custom_call_target="tpu_custom_call" | custom-call | tf_op jit(solution)/shard_map/pallas_call | solution.py:575
  (3 shorter events, 0.0 us)
Async XLA Ops:
  2.8 42.6 %all-to-all-start = ((f32[32,16,128]{2,1,0:T(8,128)}), f32[32,16,128]{2,1,0:T(8,128)S(1)}, u32[]{:S(2)}, u32[]{:S(2)}) async-start(f32[32,16,128]{2,1,0:T(8,128)} %shard_map.63), calls=%async_computation | async-start | bytes 524288 | tf_op jit(solution)/shard_map/all_to_all | solution.py:533
  17.9 5.9 %collective-permute-start = (f32[32,128]{1,0:T(8,128)S(1)}, f32[32,128]{1,0:T(8,128)S(1)}, u32[]{:S(2)}, u32[]{:S(2)}) collective-permute-start(f32[32,128]{1,0:T(8,128)S(1)} %get-tuple-element.13.mine_ref), channel_id=1, source_target_pairs={{0,1},{2,3},{4,5},{6,7},{8,9},{10,11},{12,13},{14,15},{1,0},{3,2},... | collective-permute-start | bytes 49160 | tf_op jit(solution)/shard_map/ppermute | solution.py:512
  23.9 6.6 %collective-permute-start.1 = (f32[32,128]{1,0:T(8,128)S(1)}, f32[32,128]{1,0:T(8,128)S(1)}, u32[]{:S(2)}, u32[]{:S(2)}) collective-permute-start(f32[32,128]{1,0:T(8,128)S(1)} %shard_map.60), channel_id=1, source_target_pairs={{1,16},{17,32},{33,48},{49,64},{65,80},{81,96},{97,112},{113,128},... | collective-permute-start | bytes 49160 | tf_op jit(solution)/shard_map/ppermute | solution.py:532
  30.5 14.9 %collective-permute-start.2 = (f32[32,128]{1,0:T(8,128)S(1)}, f32[32,128]{1,0:T(8,128)S(1)}, u32[]{:S(2)}, u32[]{:S(2)}) collective-permute-start(f32[32,128]{1,0:T(8,128)S(1)} %collective-permute-done.1.near_ref), channel_id=1, source_target_pairs={{0,1},{2,3},{4,5},{6,7},{8,9},{10,11},{12,13},{14,15},{1,0},{3,2},... | collective-permute-start | bytes 49160 | tf_op jit(solution)/shard_map/ppermute | solution.py:534
  32.4 13.0 %collective-permute-start.3 = (f32[3,8,128]{2,1,0:T(8,128)S(1)}, f32[3,8,128]{2,1,0:T(8,128)S(1)}, u32[]{:S(2)}, u32[]{:S(2)}) collective-permute-start(f32[3,8,128]{2,1,0:T(8,128)S(1)} %get-tuple-element.14), channel_id=1, source_target_pairs={{1,2},{3,4},{5,6},{7,8},{9,10},{11,12},{13,14},{2,1},{4,3},{6,5},{... | collective-permute-start | bytes 36872 | tf_op jit(solution)/shard_map/ppermute | solution.py:542
  40.5 4.9 %collective-permute-start.4 = (f32[8,128]{1,0:T(8,128)S(1)}, f32[8,128]{1,0:T(8,128)S(1)}, u32[]{:S(2)}, u32[]{:S(2)}) collective-permute-start(f32[8,128]{1,0:T(8,128)S(1)} %get-tuple-element.15), channel_id=1, source_target_pairs={{0,2},{2,4},{4,6},{6,8},{8,10},{10,12},{12,14},{3,1},{5,3},{7,5},{... | collective-permute-start | bytes 12296 | tf_op jit(solution)/shard_map/ppermute | solution.py:543
  48.5 5.9 %collective-permute-start.5 = (f32[2,8,128]{2,1,0:T(8,128)S(1)}, f32[2,8,128]{2,1,0:T(8,128)S(1)}, u32[]{:S(2)}, u32[]{:S(2)}) collective-permute-start(f32[2,8,128]{2,1,0:T(8,128)S(1)} %get-tuple-element.23), channel_id=1, source_target_pairs={{1,2},{3,4},{5,6},{7,8},{9,10},{11,12},{13,14},{2,1},{4,3},{6,5},{... | collective-permute-start | bytes 24584 | tf_op jit(solution)/shard_map/ppermute | solution.py:566
  54.4 4.5 %collective-permute-start.6 = (f32[32,128]{1,0:T(8,128)S(1)}, f32[32,128]{1,0:T(8,128)S(1)}, u32[]{:S(2)}, u32[]{:S(2)}) collective-permute-start(f32[32,128]{1,0:T(8,128)S(1)} %shard_map.65), channel_id=1, source_target_pairs={{0,1},{2,3},{4,5},{6,7},{8,9},{10,11},{12,13},{14,15},{1,0},{3,2},... | collective-permute-start | bytes 49160 | tf_op jit(solution)/shard_map/ppermute | solution.py:574
where the time goes:
time: 59.9 us; the launch traced here: 59.6 us
  starting transfers between devices  36 us (60%)
  waiting for transfers between devices  16.7 us (28%)
  Pallas kernels  5.92 us (10%)
  between operations  0.75 us (1%)
    all_to_all x1, starting transfers between devices, body(): got = lax.all_to_all(sent, 'illum', 0, 0, tiled=True)  15.1 us
    ppermute x1, starting transfers between devices, body(): across_part = lax.ppermute(across_part, rows_axis, across)  8.07 us
    ppermute x1, waiting for transfers between devices, body(): near = lax.ppermute(near, ('illum', 'cuts'), beside)  4.35 us
    ppermute x1, waiting for transfers between devices, body(): edges = lax.ppermute(edges, rows_axis, across)  3.94 us
    pallas_call x1, Pallas kernels, body(): pl.pallas_call(march, out_shape=(f32(32, 128), f32(32, 128), f32(2, 8, 12...  3.07 us
    ppermute x1, waiting for transfers between devices, body(): along_part = lax.ppermute(along_part, rows_axis, along)  3 us
    ppermute x1, starting transfers between devices, body(): other = lax.ppermute(mine, rows_axis, partner)  2.98 us
    ppermute x1, waiting for transfers between devices, body(): other = lax.ppermute(mine, rows_axis, partner)  2.88 us
  transfers between devices with their start and end apart: 8, of which 5 were waited for; matrix products, arithmetic and copies ran while one was open for 0% of the time, Pallas kernels for 0%

commit v1 on v0

--- a/solution.py
+++ b/solution.py
@@ -203,20 +203,13 @@
         copy.wait()
 
 
-def march(
-    place_ref, here_ref, left_ref, right_ref, got_ref,
-    mine_ref, other_ref, edge_ref,
-    table, flat, field, stored, sums,
-):
+def transmit(place_ref, here_ref, left_ref, right_ref, table, flat):
+    sub = lax.broadcasted_iota(jnp.int32, (8, 128), 0)
     block, slab, cut = place_ref[0], place_ref[1], place_ref[2]
-    first = cut == 0
     lane = lanes_of((8, 128))
-    sub = lax.broadcasted_iota(jnp.int32, (8, 128), 0)
     upper = lane < 64
     window = jnp.bitwise_and(lane, 63)
-    half = jnp.bitwise_and(lane, 64)
     place = jnp.bitwise_and(lane, 15)
-    group = jnp.bitwise_and(lane // 16, 3)
     top = 32 * slab + 16 * cut - HALO
     left_column = 32 * block - REACH
 
@@ -263,6 +256,26 @@
     for m in range(4):
         table[0:8, m] = wide[:, 128 * m : 128 * m + 128].reshape(8, 16, 128)
 
+
+def march(
+    place_ref, table, got_ref,
+    mine_ref, other_ref, edge_ref,
+    flat, field, stored, sums,
+):
+    block, slab, cut = place_ref[0], place_ref[1], place_ref[2]
+    first = cut == 0
+    lane = lanes_of((8, 128))
+    upper = lane < 64
+    window = jnp.bitwise_and(lane, 63)
+    half = jnp.bitwise_and(lane, 64)
+    place = jnp.bitwise_and(lane, 15)
+    group = jnp.bitwise_and(lane // 16, 3)
+    top = 32 * slab + 16 * cut - HALO
+    left_column = 32 * block - REACH
+
+    def columns(m):
+        return left_column + 4 * place + m
+
     def spread(n, m, r):
         return jnp.broadcast_to(table[n, m, r : r + 1], (8, 128))
 
@@ -549,20 +562,27 @@
         compiler_params=small,
     )(place, mine, other, near, far, across_part, along_part)
 
+    table = pl.pallas_call(
+        transmit,
+        out_shape=f32(9, 4, 16, 128),
+        in_specs=[VMEM] * 4,
+        out_specs=VMEM,
+        scratch_shapes=[pltpu.VMEM((128, 128), jnp.float32)],
+        compiler_params=small,
+    )(place, here, from_left, from_right)
     mine, other, edges = pl.pallas_call(
         march,
         out_shape=(f32(32, 128), f32(32, 128), f32(2, 8, 128)),
-        in_specs=[VMEM] * 5,
+        in_specs=[VMEM] * 3,
         out_specs=(VMEM,) * 3,
         scratch_shapes=[
-            pltpu.VMEM((9, 4, 16, 128), jnp.float32),
             pltpu.VMEM((128, 128), jnp.float32),
             pltpu.VMEM((2, 16, 4, 8, 128), jnp.float32),
             pltpu.VMEM((8, 16, 4, 8, 128), jnp.float32),
             pltpu.VMEM((8, 4, 16, 128), jnp.float32),
         ],
         compiler_params=large,
-    )(place, here, from_left, from_right, got.reshape(512, 128))
+    )(place, table, got.reshape(512, 128))
     edges = lax.ppermute(edges, rows_axis, across)
     other = pl.pallas_call(
         add_edges,

time: 59.9 us -> 60.2 us (level)
  transfers between devices with their start and end apart: 8 -> 8, of which waited for: 5 -> 5; matrix products, arithmetic and copies ran while one was open for 0% -> 0% of each run, Pallas kernels for 0% -> 1%
where the time goes in v1:
time: 60.2 us; the launch traced here: 59.8 us
  starting transfers between devices  36 us (60%)
  waiting for transfers between devices  16.7 us (28%)
  Pallas kernels  6.14 us (10%)
  between operations  0.76 us (1%)
    all_to_all x1, starting transfers between devices, body(): got = lax.all_to_all(sent, 'illum', 0, 0, tiled=True)  15.1 us
    ppermute x1, starting transfers between devices, body(): across_part = lax.ppermute(across_part, rows_axis, across)  8.07 us
    ppermute x1, waiting for transfers between devices, body(): near = lax.ppermute(near, ('illum', 'cuts'), beside)  4.35 us
    ppermute x1, waiting for transfers between devices, body(): edges = lax.ppermute(edges, rows_axis, across)  3.94 us
    ppermute x1, waiting for transfers between devices, body(): along_part = lax.ppermute(along_part, rows_axis, along)  3 us
    ppermute x1, starting transfers between devices, body(): other = lax.ppermute(mine, rows_axis, partner)  2.98 us
    ppermute x1, waiting for transfers between devices, body(): other = lax.ppermute(mine, rows_axis, partner)  2.88 us
    pallas_call x1, Pallas kernels, body(): pl.pallas_call(march, out_shape=(f32(32, 128), f32(32, 128), f32(2, 8, 12...  2.86 us
  transfers between devices with their start and end apart: 8, of which 5 were waited for; matrix products, arithmetic and copies ran while one was open for 0% of the time, Pallas kernels for 1%

profile of v1, /device:TPU:57, one launch (start us, length us, event | category | flops | bytes accessed | tf_op | source)
XLA Modules:
  0.0 59.8 jit_solution(13386789849212067053)
XLA Ops:
  0.6 0.1 add_add_fusion
  0.7 1.0 %shard_map.59 = (f32[32,128]{1,0:T(8,128)S(1)}, f32[2,32,1024]{2,1,0:T(8,128)S(1)}, f32[8,128]{1,0:T(8,128)S(1)}) custom-call(f32[2,32,32]{2,1,0:T(8,128)} %phase_ref.1, f32[2,32,32]{2,1,0:T(8,128)} %atten_ref.1, f32[1,2,32,1024]{3,2,1,0:T(8,128)} %measured_ref.1, s32[1,2]{1,0:T(1,128)} %angles_ref.1), custom_call_target="tpu_custom_call" | custom-call | tf_op jit(solution)/shard_map/pallas_call | solution.py:512
  1.7 0.1 broadcast.4.place_ref
  1.8 1.0 %shard_map.64 = f32[32,16,128]{2,1,0:T(8,128)} custom-call(s32[3,8,128]{2,1,0:T(8,128)S(1)} %broadcast.4.place_ref, f32[2,32,1024]{2,1,0:T(8,128)S(1)} %get-tuple-element.19.whole_ref, f32[8,128]{1,0:T(8,128)S(1)} %get-tuple-element.20.head_ref), custom_call_target="tpu_custom_call" | custom-call | tf_op jit(solution)/shard_map/pallas_call | solution.py:526
  2.8 15.1 %all-to-all-start = ((f32[32,16,128]{2,1,0:T(8,128)}), f32[32,16,128]{2,1,0:T(8,128)S(1)}, u32[]{:S(2)}, u32[]{:S(2)}) async-start(f32[32,16,128]{2,1,0:T(8,128)} %shard_map.64), calls=%async_computation | async-start | bytes 524288 | tf_op jit(solution)/shard_map/all_to_all | solution.py:546
  17.9 3.0 %collective-permute-start = (f32[32,128]{1,0:T(8,128)S(1)}, f32[32,128]{1,0:T(8,128)S(1)}, u32[]{:S(2)}, u32[]{:S(2)}) collective-permute-start(f32[32,128]{1,0:T(8,128)S(1)} %get-tuple-element.13.mine_ref), channel_id=1, source_target_pairs={{0,1},{2,3},{4,5},{6,7},{8,9},{10,11},{12,13},{14,15},{1,0},{3,2},... | collective-permute-start | bytes 49160 | tf_op jit(solution)/shard_map/ppermute | solution.py:525
  20.9 2.9 %collective-permute-done.other_ref = f32[32,128]{1,0:T(8,128)S(1)} collective-permute-done((f32[32,128]{1,0:T(8,128)S(1)}, f32[32,128]{1,0:T(8,128)S(1)}, u32[]{:S(2)}, u32[]{:S(2)}) %collective-permute-start) | collective-permute-done | bytes 16416 | tf_op jit(solution)/shard_map/ppermute | solution.py:525
  23.8 0.1 shard_map.60
  23.9 2.2 %collective-permute-start.1 = (f32[32,128]{1,0:T(8,128)S(1)}, f32[32,128]{1,0:T(8,128)S(1)}, u32[]{:S(2)}, u32[]{:S(2)}) collective-permute-start(f32[32,128]{1,0:T(8,128)S(1)} %shard_map.60), channel_id=1, source_target_pairs={{1,16},{17,32},{33,48},{49,64},{65,80},{81,96},{97,112},{113,128},... | collective-permute-start | bytes 49160 | tf_op jit(solution)/shard_map/ppermute | solution.py:545
  26.1 4.3 %collective-permute-done.1.near_ref = f32[32,128]{1,0:T(8,128)S(1)} collective-permute-done((f32[32,128]{1,0:T(8,128)S(1)}, f32[32,128]{1,0:T(8,128)S(1)}, u32[]{:S(2)}, u32[]{:S(2)}) %collective-permute-start.1) | collective-permute-done | bytes 16416 | tf_op jit(solution)/shard_map/ppermute | solution.py:545
  30.5 1.9 %collective-permute-start.2 = (f32[32,128]{1,0:T(8,128)S(1)}, f32[32,128]{1,0:T(8,128)S(1)}, u32[]{:S(2)}, u32[]{:S(2)}) collective-permute-start(f32[32,128]{1,0:T(8,128)S(1)} %collective-permute-done.1.near_ref), channel_id=1, source_target_pairs={{0,1},{2,3},{4,5},{6,7},{8,9},{10,11},{12,13},{14,15},{1,0},{3,2},... | collective-permute-start | bytes 49160 | tf_op jit(solution)/shard_map/ppermute | solution.py:547
  32.4 8.1 %collective-permute-start.3 = (f32[3,8,128]{2,1,0:T(8,128)S(1)}, f32[3,8,128]{2,1,0:T(8,128)S(1)}, u32[]{:S(2)}, u32[]{:S(2)}) collective-permute-start(f32[3,8,128]{2,1,0:T(8,128)S(1)} %get-tuple-element.14), channel_id=1, source_target_pairs={{1,2},{3,4},{5,6},{7,8},{9,10},{11,12},{13,14},{2,1},{4,3},{6,5},{... | collective-permute-start | bytes 36872 | tf_op jit(solution)/shard_map/ppermute | solution.py:555
  40.5 1.9 %collective-permute-start.4 = (f32[8,128]{1,0:T(8,128)S(1)}, f32[8,128]{1,0:T(8,128)S(1)}, u32[]{:S(2)}, u32[]{:S(2)}) collective-permute-start(f32[8,128]{1,0:T(8,128)S(1)} %get-tuple-element.15), channel_id=1, source_target_pairs={{0,2},{2,4},{4,6},{6,8},{8,10},{10,12},{12,14},{3,1},{5,3},{7,5},{... | collective-permute-start | bytes 12296 | tf_op jit(solution)/shard_map/ppermute | solution.py:556
  42.4 3.0 %collective-permute-done.4.along_ref = f32[8,128]{1,0:T(8,128)S(1)} collective-permute-done((f32[8,128]{1,0:T(8,128)S(1)}, f32[8,128]{1,0:T(8,128)S(1)}, u32[]{:S(2)}, u32[]{:S(2)}) %collective-permute-start.4) | collective-permute-done | bytes 4128 | tf_op jit(solution)/shard_map/ppermute | solution.py:556
  45.4 0.0 collective-permute-done.3.across_ref
  45.4 0.0 collective-permute-done.2.far_ref
  45.4 0.4 shard_map.63.table
  45.9 0.0 all-to-all-done
  45.9 2.9 %shard_map.65 = (f32[32,128]{1,0:T(8,128)S(1)}, f32[32,128]{1,0:T(8,128)S(1)}, f32[2,8,128]{2,1,0:T(8,128)S(1)}) custom-call(s32[3,8,128]{2,1,0:T(8,128)S(1)} %broadcast.4.place_ref, f32[9,4,16,128]{3,2,1,0:T(8,128)S(1)} %shard_map.63.table, f32[512,128]{1,0:T(8,128)S(1)} %bitcast.4), custom_call_target="tpu_custom_call" | custom-call | tf_op jit(solution)/shard_map/pallas_call | solution.py:573
  48.7 1.9 %collective-permute-start.5 = (f32[2,8,128]{2,1,0:T(8,128)S(1)}, f32[2,8,128]{2,1,0:T(8,128)S(1)}, u32[]{:S(2)}, u32[]{:S(2)}) collective-permute-start(f32[2,8,128]{2,1,0:T(8,128)S(1)} %get-tuple-element.23), channel_id=1, source_target_pairs={{1,2},{3,4},{5,6},{7,8},{9,10},{11,12},{13,14},{2,1},{4,3},{6,5},{... | collective-permute-start | bytes 24584 | tf_op jit(solution)/shard_map/ppermute | solution.py:586
  50.7 3.9 %collective-permute-done.5.edge_ref = f32[2,8,128]{2,1,0:T(8,128)S(1)} collective-permute-done((f32[2,8,128]{2,1,0:T(8,128)S(1)}, f32[2,8,128]{2,1,0:T(8,128)S(1)}, u32[]{:S(2)}, u32[]{:S(2)}) %collective-permute-start.5) | collective-permute-done | bytes 8224 | tf_op jit(solution)/shard_map/ppermute | solution.py:586
  54.6 1.9 %collective-permute-start.6 = (f32[32,128]{1,0:T(8,128)S(1)}, f32[32,128]{1,0:T(8,128)S(1)}, u32[]{:S(2)}, u32[]{:S(2)}) collective-permute-start(f32[32,128]{1,0:T(8,128)S(1)} %shard_map.66), channel_id=1, source_target_pairs={{0,1},{2,3},{4,5},{6,7},{8,9},{10,11},{12,13},{14,15},{1,0},{3,2},... | collective-permute-start | bytes 49160 | tf_op jit(solution)/shard_map/ppermute | solution.py:594
  56.5 2.6 %collective-permute-done.6.other_ref = f32[32,128]{1,0:T(8,128)S(1)} collective-permute-done((f32[32,128]{1,0:T(8,128)S(1)}, f32[32,128]{1,0:T(8,128)S(1)}, u32[]{:S(2)}, u32[]{:S(2)}) %collective-permute-start.6) | collective-permute-done | bytes 16416 | tf_op jit(solution)/shard_map/ppermute | solution.py:594
  59.1 0.7 %shard_map.67 = (f32[2,32,32]{2,1,0:T(8,128)}, f32[2,32,32]{2,1,0:T(8,128)}) custom-call(s32[3,8,128]{2,1,0:T(8,128)S(1)} %broadcast.4.place_ref, f32[32,128]{1,0:T(8,128)S(1)} %get-tuple-element.21.mine_ref, f32[32,128]{1,0:T(8,128)S(1)} %collective-permute-done.6.other_ref, f32[2,8,128]{2,1,0:T(8,128)S(1)} %collective-permute-done.5.edge_ref), custom_call_target="tpu_custom_call" | custom-call | tf_op jit(solution)/shard_map/pallas_call | solution.py:595
  (3 shorter events, 0.0 us)
Async XLA Ops:
  2.8 43.0 %all-to-all-start = ((f32[32,16,128]{2,1,0:T(8,128)}), f32[32,16,128]{2,1,0:T(8,128)S(1)}, u32[]{:S(2)}, u32[]{:S(2)}) async-start(f32[32,16,128]{2,1,0:T(8,128)} %shard_map.64), calls=%async_computation | async-start | bytes 524288 | tf_op jit(solution)/shard_map/all_to_all | solution.py:546
  17.9 5.9 %collective-permute-start = (f32[32,128]{1,0:T(8,128)S(1)}, f32[32,128]{1,0:T(8,128)S(1)}, u32[]{:S(2)}, u32[]{:S(2)}) collective-permute-start(f32[32,128]{1,0:T(8,128)S(1)} %get-tuple-element.13.mine_ref), channel_id=1, source_target_pairs={{0,1},{2,3},{4,5},{6,7},{8,9},{10,11},{12,13},{14,15},{1,0},{3,2},... | collective-permute-start | bytes 49160 | tf_op jit(solution)/shard_map/ppermute | solution.py:525
  23.9 6.6 %collective-permute-start.1 = (f32[32,128]{1,0:T(8,128)S(1)}, f32[32,128]{1,0:T(8,128)S(1)}, u32[]{:S(2)}, u32[]{:S(2)}) collective-permute-start(f32[32,128]{1,0:T(8,128)S(1)} %shard_map.60), channel_id=1, source_target_pairs={{1,16},{17,32},{33,48},{49,64},{65,80},{81,96},{97,112},{113,128},... | collective-permute-start | bytes 49160 | tf_op jit(solution)/shard_map/ppermute | solution.py:545
  30.5 14.9 %collective-permute-start.2 = (f32[32,128]{1,0:T(8,128)S(1)}, f32[32,128]{1,0:T(8,128)S(1)}, u32[]{:S(2)}, u32[]{:S(2)}) collective-permute-start(f32[32,128]{1,0:T(8,128)S(1)} %collective-permute-done.1.near_ref), channel_id=1, source_target_pairs={{0,1},{2,3},{4,5},{6,7},{8,9},{10,11},{12,13},{14,15},{1,0},{3,2},... | collective-permute-start | bytes 49160 | tf_op jit(solution)/shard_map/ppermute | solution.py:547
  32.4 13.0 %collective-permute-start.3 = (f32[3,8,128]{2,1,0:T(8,128)S(1)}, f32[3,8,128]{2,1,0:T(8,128)S(1)}, u32[]{:S(2)}, u32[]{:S(2)}) collective-permute-start(f32[3,8,128]{2,1,0:T(8,128)S(1)} %get-tuple-element.14), channel_id=1, source_target_pairs={{1,2},{3,4},{5,6},{7,8},{9,10},{11,12},{13,14},{2,1},{4,3},{6,5},{... | collective-permute-start | bytes 36872 | tf_op jit(solution)/shard_map/ppermute | solution.py:555
  40.5 4.9 %collective-permute-start.4 = (f32[8,128]{1,0:T(8,128)S(1)}, f32[8,128]{1,0:T(8,128)S(1)}, u32[]{:S(2)}, u32[]{:S(2)}) collective-permute-start(f32[8,128]{1,0:T(8,128)S(1)} %get-tuple-element.15), channel_id=1, source_target_pairs={{0,2},{2,4},{4,6},{6,8},{8,10},{10,12},{12,14},{3,1},{5,3},{7,5},{... | collective-permute-start | bytes 12296 | tf_op jit(solution)/shard_map/ppermute | solution.py:556
  48.7 5.9 %collective-permute-start.5 = (f32[2,8,128]{2,1,0:T(8,128)S(1)}, f32[2,8,128]{2,1,0:T(8,128)S(1)}, u32[]{:S(2)}, u32[]{:S(2)}) collective-permute-start(f32[2,8,128]{2,1,0:T(8,128)S(1)} %get-tuple-element.23), channel_id=1, source_target_pairs={{1,2},{3,4},{5,6},{7,8},{9,10},{11,12},{13,14},{2,1},{4,3},{6,5},{... | collective-permute-start | bytes 24584 | tf_op jit(solution)/shard_map/ppermute | solution.py:586
  54.6 4.5 %collective-permute-start.6 = (f32[32,128]{1,0:T(8,128)S(1)}, f32[32,128]{1,0:T(8,128)S(1)}, u32[]{:S(2)}, u32[]{:S(2)}) collective-permute-start(f32[32,128]{1,0:T(8,128)S(1)} %shard_map.66), channel_id=1, source_target_pairs={{0,1},{2,3},{4,5},{6,7},{8,9},{10,11},{12,13},{14,15},{1,0},{3,2},... | collective-permute-start | bytes 49160 | tf_op jit(solution)/shard_map/ppermute | solution.py:594
